TPU v7x, 256 devices: a whole 4x4x8 slice. The times are simulated.
256 devices in a mesh: section: 4 (over z_hi), dp: 16 (over x, z_lo, core), feat: 4 (over y).
Axes of the slice: x: 4, y: 4, z: 8 (z_hi: 4, z_lo: 2; z = z_hi * 2 + z_lo), core: 2. Of those that a mesh axis runs over, the one named last changes fastest.
Arguments:
- tokens: bfloat16 [4096, 16384], P('dp', 'feat'), may hold values from -6 to 6
- basis: bfloat16 [2048, 16384], P('section', 'feat'), may hold values from -0.046875 to 0.046875
Outputs:
- basis_step: bfloat16 [2048, 16384], P('section', 'feat')
- projections: float32 [4096, 2048], P('dp', 'section')
All inputs are finite; a program needn't handle non-finite values.
Results may differ from a plain program's by a relative error of at most 0.034.
Values may be sent and summed in bfloat16 or wider, within the bound.
A program may use at most 64 MiB of HBM per device.

v0:
```python
import math

import jax
import jax.numpy as jnp
from jax import lax
from jax.sharding import PartitionSpec as P

D = 16384


def from_behind(block, axis, distance):
    devices = range(lax.axis_size(axis))
    route = [(i - distance, i) for i in devices if i - distance in devices]
    return lax.ppermute(block, axis, route)


def project(current, basis):
    partial_value = lax.dot_general(
        current, basis, (((1,), (1,)), ((), ())), preferred_element_type=jnp.float32
    )
    scores = lax.psum(partial_value.astype(jnp.bfloat16), "feat").astype(jnp.float32)
    rounded = scores.astype(jnp.bfloat16)
    deflated = (
        current.astype(jnp.float32) - jnp.dot(rounded, basis, preferred_element_type=jnp.float32)
    ).astype(jnp.bfloat16)
    return (scores, deflated)


def shards(tokens, basis):
    section_id = lax.axis_index("section")
    sections = lax.axis_size("section")
    row_count = tokens.shape[0]
    block_rows = basis.shape[0]
    section_input = tokens
    section_scores = jnp.zeros((row_count, block_rows), jnp.float32)
    current = tokens
    for block_id in range(sections):
        scores, deflated = project(current, basis)
        is_mine = section_id == block_id
        section_input = jnp.where(is_mine, current, section_input)
        section_scores = jnp.where(is_mine, scores, section_scores)
        if block_id + 1 < sections:
            current = from_behind(deflated, "section", 1)
    rounded = section_scores.astype(jnp.bfloat16)
    hebbian_part = lax.dot_general(
        rounded, section_input, (((0,), (0,)), ((), ())), preferred_element_type=jnp.float32
    )
    covariance_part = lax.dot_general(
        rounded, rounded, (((0,), (0,)), ((), ())), preferred_element_type=jnp.float32
    )
    scaling = math.sqrt(D) / (row_count * lax.axis_size("dp"))
    hebbian, covariance = (
        lax.psum(hebbian_part.astype(jnp.bfloat16), "dp").astype(jnp.float32),
        lax.psum(covariance_part.astype(jnp.bfloat16), "dp").astype(jnp.float32),
    )
    triangle = jnp.tril(covariance).astype(jnp.bfloat16)
    damping = jnp.dot(triangle, basis, preferred_element_type=jnp.float32)
    basis_step = ((hebbian - damping) * scaling).astype(jnp.bfloat16)
    return (basis_step, section_scores)


def solution(mesh):
    in_specs = (P("dp", "feat"), P("section", "feat"))
    out_specs = (P("section", "feat"), P("dp", "section"))
    return jax.shard_map(shards, mesh=mesh, in_specs=in_specs, out_specs=out_specs, check_vma=False)
```

profile of v0, /device:TPU:225, one launch (start us, length us, event | category | flops | bytes accessed | tf_op | source)
XLA Modules:
  0.0 668.3 jit_solution(1361341420464670958)
XLA Ops:
  7.2 0.0 copy-start.3
  7.2 0.0 all-reduce.7.cloned.1.call-start
  7.2 5.0 convolution_convert_fusion.5
  12.2 0.0 all-reduce.7.cloned.1.call-update
  12.2 0.0 all-reduce.9.cloned.1.call-start
  12.2 45.2 %all-reduce.7.cloned.1.call-done = bf16[256,512]{1,0:T(8,128)(2,1)} async-done(((bf16[256,512]{1,0:T(8,128)(2,1)}), bf16[256,512]{1,0:T(8,128)(2,1)}) %all-reduce.7.cloned.1.call-update) | async-done | bytes 262160 | tf_op jit(solution)/shard_map/psum | solution.py:21
  57.5 0.0 copy-done.3
  57.5 0.0 copy-start
  57.5 3.7 fusion
  61.1 1.3 collective-permute-start
  62.4 92.8 %collective-permute-done = bf16[256,4096]{1,0:T(8,128)(2,1)S(1)} collective-permute-done((bf16[256,4096]{1,0:T(8,128)(2,1)S(1)}, bf16[256,4096]{1,0:T(8,128)(2,1)S(1)}, u32[]{:S(2)}, u32[]{:S(2)}) %collective-permute-start) | collective-permute-done | bytes 2097184 | tf_op jit(solution)/shard_map/ppermute | solution.py:14
  155.3 0.0 copy-start.4
  155.3 1.3 copy-done.4
  156.6 0.0 copy-done
  156.6 2.0 convolution_convert_fusion.4
  158.6 0.0 all-reduce.9.cloned.1.call-update
  158.6 0.0 all-reduce.11.cloned.1.call-start
  158.7 47.7 %all-reduce.9.cloned.1.call-done = bf16[256,512]{1,0:T(8,128)(2,1)} async-done(((bf16[256,512]{1,0:T(8,128)(2,1)}), bf16[256,512]{1,0:T(8,128)(2,1)}) %all-reduce.9.cloned.1.call-update) | async-done | bytes 262160 | tf_op jit(solution)/shard_map/psum | solution.py:21
  206.3 0.0 copy-start.1
  206.3 4.3 subtract_convert_fusion.1
  210.7 1.3 collective-permute-start.1
  212.0 92.8 %collective-permute-done.1 = bf16[256,4096]{1,0:T(8,128)(2,1)S(1)} collective-permute-done((bf16[256,4096]{1,0:T(8,128)(2,1)S(1)}, bf16[256,4096]{1,0:T(8,128)(2,1)S(1)}, u32[]{:S(2)}, u32[]{:S(2)}) %collective-permute-start.1) | collective-permute-done | bytes 2097184 | tf_op jit(solution)/shard_map/ppermute | solution.py:14
  304.8 0.0 copy-start.5
  304.8 1.3 copy-done.5
  306.1 0.0 copy-done.1
  306.2 2.0 convolution_convert_fusion.3
  308.1 0.0 all-reduce.11.cloned.1.call-update
  308.2 0.0 all-reduce.13.cloned.1.call-start
  308.2 47.7 %all-reduce.11.cloned.1.call-done = bf16[256,512]{1,0:T(8,128)(2,1)} async-done(((bf16[256,512]{1,0:T(8,128)(2,1)}), bf16[256,512]{1,0:T(8,128)(2,1)}) %all-reduce.11.cloned.1.call-update) | async-done | bytes 262160 | tf_op jit(solution)/shard_map/psum | solution.py:21
  355.9 0.0 copy-start.2
  355.9 4.3 subtract_convert_fusion
  360.2 0.0 copy-start.8
  360.2 0.0 copy-start.9
  360.2 0.0 copy-start.10
  360.3 1.4 collective-permute-start.2
  361.7 92.8 %collective-permute-done.2 = bf16[256,4096]{1,0:T(8,128)(2,1)S(1)} collective-permute-done((bf16[256,4096]{1,0:T(8,128)(2,1)S(1)}, bf16[256,4096]{1,0:T(8,128)(2,1)S(1)}, u32[]{:S(2)}, u32[]{:S(2)}) %collective-permute-start.2) | collective-permute-done | bytes 2097184 | tf_op jit(solution)/shard_map/ppermute | solution.py:14
  454.5 0.0 copy-start.7
  454.5 1.4 copy-done.7
  455.9 0.0 copy-done.2
  455.9 2.0 convolution_convert_fusion.2
  457.9 0.0 all-reduce.13.cloned.1.call-update
  457.9 0.2 all-reduce.15.cloned.1.call-start
  458.1 47.5 %all-reduce.13.cloned.1.call-done = bf16[256,512]{1,0:T(8,128)(2,1)} async-done(((bf16[256,512]{1,0:T(8,128)(2,1)}), bf16[256,512]{1,0:T(8,128)(2,1)}) %all-reduce.13.cloned.1.call-update) | async-done | bytes 262160 | tf_op jit(solution)/shard_map/psum | solution.py:21
  505.6 0.0 copy-done.8
  505.6 0.0 copy-done.9
  505.6 0.0 copy-done.10
  505.6 1.1 select_select_fusion
  506.7 0.0 copy-start.6
  506.7 1.1 convolution_convert_fusion.1
  507.9 5.0 convolution_convert_fusion
  512.8 0.0 copy-done.6
  512.8 0.0 all-reduce.15.cloned.1.call-update
  512.8 140.9 %all-reduce.15.cloned.1.call-done = (bf16[512,512]{1,0:T(8,128)(2,1)}, bf16[512,4096]{1,0:T(8,128)(2,1)}) async-done(((bf16[512,512]{1,0:T(8,128)(2,1)}, bf16[512,4096]{1,0:T(8,128)(2,1)}), (bf16[512,512]{1,0:T(8,128)(2,1)}, bf16[512,4096]{1,0:T(8,128)(2,1)})) %all-reduce.15.cloned.1.call-update) | async-done | bytes 4718608 | tf_op jit(solution)/shard_map/psum | solution.py:54
  653.8 8.0 %multiply_convert_fusion = bf16[512,4096]{1,0:T(8,128)(2,1)} fusion(bf16[512,4096]{1,0:T(8,128)(2,1)} %get-tuple-element.3, bf16[512,4096]{1,0:T(8,128)(2,1)} %param.3, bf16[512,512]{1,0:T(8,128)(2,1)} %get-tuple-element.2), kind=kOutput, calls=%fused_computation | convolution fusion | flops 2156920832 | bytes 13107200 | tf_op jit(solution)/shard_map/dot_general | solution.py:57
Async XLA Ops:
  7.2 50.3 %copy-start.3 = (bf16[256,4096]{1,0:T(8,128)(2,1)S(1)}, bf16[256,4096]{1,0:T(8,128)(2,1)}, u32[]{:S(2)}) copy-start(bf16[256,4096]{1,0:T(8,128)(2,1)} %param.2) | copy-start | bytes 6291460
  7.2 50.3 %all-reduce.7.cloned.1.call-start = ((), (), s32[]{:S(2)}) async-start(), calls=%async_computation | async-start | bytes 524288 | tf_op jit(solution)/shard_map/psum | solution.py:21
  12.2 194.1 %all-reduce.9.cloned.1.call-start = ((), (), s32[]{:S(2)}) async-start(), calls=%async_computation.1 | async-start | bytes 524288 | tf_op jit(solution)/shard_map/psum | solution.py:21
  57.5 99.1 %copy-start = (bf16[512,4096]{1,0:T(8,128)(2,1)S(1)}, bf16[512,4096]{1,0:T(8,128)(2,1)}, u32[]{:S(2)}) copy-start(bf16[512,4096]{1,0:T(8,128)(2,1)} %param.3) | copy-start | bytes 12582916
  61.1 94.1 %collective-permute-start = (bf16[256,4096]{1,0:T(8,128)(2,1)S(1)}, bf16[256,4096]{1,0:T(8,128)(2,1)S(1)}, u32[]{:S(2)}, u32[]{:S(2)}) collective-permute-start(bf16[256,4096]{1,0:T(8,128)(2,1)S(1)} %fusion), channel_id=1, source_target_pairs={{0,64},{64,128},{128,192},{1,65},{65,129},{129,193},{2,66},{66,130... | collective-permute-start | bytes 6291464 | tf_op jit(solution)/shard_map/ppermute | solution.py:14
  155.3 1.3 copy-start.4
  158.6 197.3 %all-reduce.11.cloned.1.call-start = ((), (), s32[]{:S(2)}) async-start(), calls=%async_computation.2 | async-start | bytes 524288 | tf_op jit(solution)/shard_map/psum | solution.py:21
  206.3 99.8 %copy-start.1 = (bf16[512,4096]{1,0:T(8,128)(2,1)S(1)}, bf16[512,4096]{1,0:T(8,128)(2,1)}, u32[]{:S(2)}) copy-start(bf16[512,4096]{1,0:T(8,128)(2,1)} %param.3) | copy-start | bytes 12582916
  210.7 94.1 %collective-permute-start.1 = (bf16[256,4096]{1,0:T(8,128)(2,1)S(1)}, bf16[256,4096]{1,0:T(8,128)(2,1)S(1)}, u32[]{:S(2)}, u32[]{:S(2)}) collective-permute-start(bf16[256,4096]{1,0:T(8,128)(2,1)S(1)} %subtract_convert_fusion.1), channel_id=1, source_target_pairs={{0,64},{64,128},{128,192},{1,65},{65,129},{129,193},{2,66},{66,130... | collective-permute-start | bytes 6291464 | tf_op jit(solution)/shard_map/ppermute | solution.py:14
  304.8 1.3 copy-start.5
  308.2 197.4 %all-reduce.13.cloned.1.call-start = ((), (), s32[]{:S(2)}) async-start(), calls=%async_computation.3 | async-start | bytes 524288 | tf_op jit(solution)/shard_map/psum | solution.py:21
  355.9 100.0 %copy-start.2 = (bf16[512,4096]{1,0:T(8,128)(2,1)S(1)}, bf16[512,4096]{1,0:T(8,128)(2,1)}, u32[]{:S(2)}) copy-start(bf16[512,4096]{1,0:T(8,128)(2,1)} %param.3) | copy-start | bytes 12582916
  360.2 145.4 %copy-start.8 = (bf16[256,512]{1,0:T(8,128)(2,1)S(1)}, bf16[256,512]{1,0:T(8,128)(2,1)}, u32[]{:S(2)}) copy-start(bf16[256,512]{1,0:T(8,128)(2,1)} %all-reduce.7.cloned.1.call-done) | copy-start | bytes 786436
  360.2 145.4 %copy-start.9 = (bf16[256,512]{1,0:T(8,128)(2,1)S(1)}, bf16[256,512]{1,0:T(8,128)(2,1)}, u32[]{:S(2)}) copy-start(bf16[256,512]{1,0:T(8,128)(2,1)} %all-reduce.9.cloned.1.call-done) | copy-start | bytes 786436
  360.2 145.4 %copy-start.10 = (bf16[256,512]{1,0:T(8,128)(2,1)S(1)}, bf16[256,512]{1,0:T(8,128)(2,1)}, u32[]{:S(2)}) copy-start(bf16[256,512]{1,0:T(8,128)(2,1)} %all-reduce.11.cloned.1.call-done) | copy-start | bytes 786436
  360.3 94.3 %collective-permute-start.2 = (bf16[256,4096]{1,0:T(8,128)(2,1)S(1)}, bf16[256,4096]{1,0:T(8,128)(2,1)S(1)}, u32[]{:S(2)}, u32[]{:S(2)}) collective-permute-start(bf16[256,4096]{1,0:T(8,128)(2,1)S(1)} %subtract_convert_fusion), channel_id=1, source_target_pairs={{0,64},{64,128},{128,192},{1,65},{65,129},{129,193},{2,66},{66,130... | collective-permute-start | bytes 6291464 | tf_op jit(solution)/shard_map/ppermute | solution.py:14
  454.5 1.4 copy-start.7
  457.9 195.9 %all-reduce.15.cloned.1.call-start = ((), (), s32[]{:S(2)}) async-start(), calls=%async_computation.4 | async-start | bytes 9437184 | tf_op jit(solution)/shard_map/psum | solution.py:54
  506.7 6.1 copy-start.6
Sparse Core Ops, SparseCore 0:
  12.3 45.0 all-reduce.6
  158.7 47.5 all-reduce.8
  308.3 47.5 all-reduce.10
  458.0 47.5 all-reduce.12
  513.0 140.7 all-reduce.14
where the time goes:
time: 676 us; the launch traced here: 668 us
  waiting for transfers between devices  607 us (90%)
  matrix products  37.4 us (6%)
  between operations  13.9 us (2%)
    ppermute x3, waiting for transfers between devices, from_behind(): return lax.ppermute(block, axis, route)  278 us
    psum x4, waiting for transfers between devices, project(): lax.psum(partial_value.astype(jnp.bfloat16), 'feat').astype(jnp.float32)  188 us
    psum x1, waiting for transfers between devices, shards(): lax.psum(covariance_part.astype(jnp.bfloat16), 'dp').astype(jnp.float32)  141 us
  transfers between devices with their start and end apart: 8, of which 8 were waited for; matrix products, arithmetic and copies ran while one was open for 0% of the time, Pallas kernels for 0%

commit v1 on v0

v1 whole, which is shorter than its diff:
```python
import math

import jax
import jax.numpy as jnp
from jax import lax
from jax.sharding import PartitionSpec as P

D = 16384
BF16 = jnp.bfloat16
F32 = jnp.float32


def dot(a, b, ca, cb):
    return lax.dot_general(a, b, (((ca,), (cb,)), ((), ())), preferred_element_type=F32)


def shards(tokens, basis):
    s = lax.axis_index("section")
    d = lax.axis_index("dp")
    n_sec = lax.axis_size("section")
    n_dp = lax.axis_size("dp")
    rows, width = tokens.shape
    block = basis.shape[0]
    piece = block // n_dp
    scaling = math.sqrt(D) / (rows * n_dp)

    mine = lax.dynamic_slice_in_dim(basis, d * piece, piece, 0)
    slices = lax.all_gather(mine, "section").reshape(n_sec * piece, width)
    cross = dot(slices, basis, 1, 1).astype(BF16)
    cross = lax.psum(cross, "feat")
    cross = lax.all_gather(cross, ("section", "dp"))
    cross = cross.reshape(n_sec, n_dp, n_sec, piece, block)
    cross = cross.transpose(0, 2, 1, 3, 4).reshape(n_sec, n_sec, block, block)

    scores = dot(tokens, basis, 1, 1).astype(BF16)
    scores = lax.psum_scatter(scores, "feat", scatter_dimension=0, tiled=True)
    scores = lax.all_gather(scores, "section")
    rounded = []
    for b in range(n_sec):
        y = scores[b].astype(F32)
        for j in range(b):
            y = y - dot(rounded[j], cross[b, j], 1, 0)
        rounded.append(y.astype(BF16))
    q = jnp.stack(rounded)
    q = lax.all_gather(q, "feat", axis=1, tiled=True)
    q_mine = lax.dynamic_index_in_dim(q, s, 0, keepdims=False)
    projections = q_mine.astype(F32)

    gram = jnp.einsum("jrc,rk->jck", q, q_mine, preferred_element_type=F32)
    gram = gram.astype(BF16).reshape(n_sec, n_dp, piece, block).transpose(1, 0, 2, 3)
    gram = lax.psum_scatter(gram, "dp", scatter_dimension=0, tiled=True)[0]
    col = d * piece + lax.broadcasted_iota(jnp.int32, (n_sec, piece, block), 1)
    row = lax.broadcasted_iota(jnp.int32, (n_sec, piece, block), 2)
    j = lax.broadcasted_iota(jnp.int32, (n_sec, piece, block), 0)
    keep = (j < s) | ((j == s) & (col <= row))
    gram = jnp.where(keep, gram, jnp.zeros_like(gram)).reshape(n_sec * piece, block)
    part = dot(q_mine, tokens, 0, 0) - dot(gram, slices, 0, 0)
    total = lax.psum(part.astype(BF16), "dp")
    basis_step = (total.astype(F32) * scaling).astype(BF16)
    return basis_step, projections


def solution(mesh):
    in_specs = (P("dp", "feat"), P("section", "feat"))
    out_specs = (P("section", "feat"), P("dp", "section"))
    return jax.shard_map(shards, mesh=mesh, in_specs=in_specs, out_specs=out_specs, check_vma=False)
```

time: 676 us -> 517 us (0.76)
  waiting for transfers between devices: 607 us -> 439 us
  matrix products: 37.4 us -> 24.5 us
  blocking collectives: 0 us -> 11.6 us
  local copies, waits for them, and re-layouts: 4.05 us -> 11.7 us
    ppermute x3 -> x0, waiting for transfers between devices: 278 us -> none  [from_behind(): return lax.ppermute(block, axis, route)]
    all_gather x0 -> x3, waiting for transfers between devices: none -> 172 us  [the longest x1 112 us: shards(): cross = lax.all_gather(cross, ('section', 'dp'))]
    psum x5 -> x2, waiting for transfers between devices: 329 us -> 179 us  [the longest x1 139 us: shards(): total = lax.psum(part.astype(BF16), 'dp')]
    reduce_scatter x0 -> x2, waiting for transfers between devices: none -> 88.4 us  [the longest x1 61.7 us: shards(): gram = lax.psum_scatter(gram, 'dp', scatter_dimension=0, tiled=True)[0]]
    dot_general x10 -> x11, matrix products: 37.4 us -> 24.5 us  [the longest x10 22.5 us: dot(): lax.dot_general(a, b, (((ca,), (cb,)), ((), ())), preferred_element_type=...]
    all_gather x0 -> x1, blocking collectives: none -> 11.6 us  [shards(): scores = lax.all_gather(scores, 'section')]
    transpose x0 -> x1, local copies, waits for them, and re-layouts: none -> 8.28 us  [shards(): cross = cross.transpose(0, 2, 1, 3, 4).reshape(n_sec, n_sec, block, block)]
  transfers between devices with their start and end apart: 8 -> 7, of which waited for: 8 -> 7; matrix products, arithmetic and copies ran while one was open for 0% -> 1% of each run, Pallas kernels for 0% -> 0%
where the time goes in v1:
time: 517 us; the launch traced here: 508 us
  waiting for transfers between devices  439 us (85%)
  matrix products  24.5 us (5%)
  between operations  14.2 us (3%)
  local copies, waits for them, and re-layouts  11.7 us (2%)
  blocking collectives  11.6 us (2%)
  other arithmetic  6.85 us (1%)
    psum x1, waiting for transfers between devices, shards(): total = lax.psum(part.astype(BF16), 'dp')  139 us
    all_gather x1, waiting for transfers between devices, shards(): cross = lax.all_gather(cross, ('section', 'dp'))  112 us
    reduce_scatter x1, waiting for transfers between devices, shards(): gram = lax.psum_scatter(gram, 'dp', scatter_dimension=0, tiled=True)[0]  61.7 us
    psum x1, waiting for transfers between devices, shards(): cross = lax.psum(cross, 'feat')  39.5 us
    all_gather x1, waiting for transfers between devices, shards(): slices = lax.all_gather(mine, 'section').reshape(n_sec * piece, width)  35.2 us
    reduce_scatter x1, waiting for transfers between devices, shards(): scores = lax.psum_scatter(scores, 'feat', scatter_dimension=0, tiled=True)  26.7 us
    all_gather x1, waiting for transfers between devices, shards(): q = lax.all_gather(q, 'feat', axis=1, tiled=True)  24.5 us
    dot_general x10, matrix products, dot(): lax.dot_general(a, b, (((ca,), (cb,)), ((), ())), preferred_element_type=...  22.5 us
  transfers between devices with their start and end apart: 7, of which 7 were waited for; matrix products, arithmetic and copies ran while one was open for 1% of the time, Pallas kernels for 0%

profile of v1, /device:TPU:225, one launch (start us, length us, event | category | flops | bytes accessed | tf_op | source)
XLA Modules:
  0.0 508.4 jit_solution(6253353343966309557)
XLA Ops:
  7.2 0.0 copy-start
  7.2 0.0 all-gather.10.cloned.1.call-start
  7.2 1.8 constant_dynamic-slice_fusion
  9.0 0.0 all-gather.10.cloned.1.call-update
  9.1 0.0 all-reduce.3.cloned.1.call-start
  9.1 35.2 %all-gather.10.cloned.1.call-done = bf16[128,4096]{1,0:T(8,128)(2,1)} async-done(((bf16[32,4096]{1,0:T(8,128)(2,1)}), bf16[128,4096]{1,0:T(8,128)(2,1)}) %all-gather.10.cloned.1.call-update) | async-done | bytes 1048592 | tf_op jit(solution)/shard_map/all_gather | solution.py:28
  44.3 4.7 fusion.1
  49.0 0.0 all-reduce.3.cloned.1.call-update
  49.1 0.0 reduce-scatter.3.cloned.1.call-start
  49.1 0.0 copy-done
  49.1 4.2 convolution_convert_fusion.1
  53.3 0.0 reduce-scatter.3.cloned.1.call-update
  53.3 0.0 all-gather.6.cloned.1.call-start
  53.4 39.5 %all-reduce.3.cloned.1.call-done = bf16[1,128,512]{2,1,0:T(8,128)(2,1)} async-done(((bf16[1,128,512]{2,1,0:T(8,128)(2,1)}), bf16[1,128,512]{2,1,0:T(8,128)(2,1)}) %all-reduce.3.cloned.1.call-update) | async-done | bytes 131088 | tf_op jit(solution)/shard_map/psum | solution.py:30
  92.9 0.0 all-gather.6.cloned.1.call-update
  92.9 0.0 all-gather.8.cloned.1.call-start
  93.0 26.7 %reduce-scatter.3.cloned.1.call-done = bf16[64,512]{1,0:T(8,128)(2,1)} async-done(((bf16[256,512]{1,0:T(8,128)(2,1)}), bf16[64,512]{1,0:T(8,128)(2,1)}) %reduce-scatter.3.cloned.1.call-update) | async-done | bytes 65552 | tf_op jit(solution)/shard_map/reduce_scatter | solution.py:36
  119.6 11.6 %all-gather = bf16[256,512]{1,0:T(8,128)(2,1)S(1)} all-gather(bf16[64,512]{1,0:T(8,128)(2,1)} %reduce-scatter.3.cloned.1.call-done), channel_id=2, replica_groups=mesh['section'=4,'dp'=16,'feat'=4] {'section'}, dimensions={0}, use_global_device_ids=true | all-gather | bytes 327680 | tf_op jit(solution)/shard_map/all_gather | solution.py:37
  131.2 112.4 %all-gather.6.cloned.1.call-done = bf16[64,128,512]{2,1,0:T(8,128)(2,1)} async-done(((bf16[1,128,512]{2,1,0:T(8,128)(2,1)}), bf16[64,128,512]{2,1,0:T(8,128)(2,1)}) %all-gather.6.cloned.1.call-update) | async-done | bytes 8388624 | tf_op jit(solution)/shard_map/all_gather | solution.py:31
  243.7 8.3 %copy.8 = bf16[4,4,16,32,512]{4,3,2,1,0:T(8,128)(2,1)} copy(bf16[4,4,16,32,512]{4,3,1,2,0:T(8,128)(2,1)} %bitcast.67) | data formatting | bytes 16777216 | tf_op jit(solution)/shard_map/transpose | solution.py:33
  251.9 1.2 fusion.2
  253.2 1.2 convolution_subtract_fusion.4
  254.4 1.2 convolution_subtract_fusion.2
  255.7 1.2 fusion.3
  256.9 1.2 convolution_subtract_fusion.1
  258.2 1.2 fusion.5
  259.4 0.7 pad_maximum_fusion
  260.2 0.0 all-gather.8.cloned.1.call-update
  260.2 0.0 reduce-scatter.5.cloned.1.call-start
  260.3 24.5 %all-gather.8.cloned.1.call-done = bf16[4,256,512]{2,1,0:T(8,128)(2,1)} async-done(((bf16[4,64,512]{2,1,0:T(8,128)(2,1)}), bf16[4,256,512]{2,1,0:T(8,128)(2,1)}) %all-gather.8.cloned.1.call-update) | async-done | bytes 1048592 | tf_op jit(solution)/shard_map/all_gather | solution.py:45
  284.8 2.0 convolution_convert_fusion
  286.8 1.6 copy.11
  288.3 0.0 reduce-scatter.5.cloned.1.call-update
  288.3 0.0 all-reduce.5.cloned.1.call-start
  288.4 61.7 %reduce-scatter.5.cloned.1.call-done = bf16[1,4,32,512]{3,2,1,0:T(8,128)(2,1)} async-done(((bf16[16,4,32,512]{3,2,1,0:T(8,128)(2,1)}), bf16[1,4,32,512]{3,2,1,0:T(8,128)(2,1)}) %reduce-scatter.5.cloned.1.call-update) | async-done | bytes 131088 | tf_op jit(solution)/shard_map/reduce_scatter | solution.py:51
  350.1 0.0 copy-start.1
  350.1 2.7 fusion.13
  352.9 0.0 copy-done.1
  352.9 3.4 fusion
  356.3 0.0 all-reduce.5.cloned.1.call-update
  356.3 0.9 bitcast_convert_fusion
  357.2 139.2 %all-reduce.5.cloned.1.call-done = bf16[512,4096]{1,0:T(8,128)(2,1)} async-done(((bf16[512,4096]{1,0:T(8,128)(2,1)}), bf16[512,4096]{1,0:T(8,128)(2,1)}) %all-reduce.5.cloned.1.call-update) | async-done | bytes 4194320 | tf_op jit(solution)/shard_map/psum | solution.py:58
  496.4 5.2 %multiply_convert_fusion = bf16[512,4096]{1,0:T(8,128)(2,1)} fusion(bf16[512,4096]{1,0:T(8,128)(2,1)} %all-reduce.5.cloned.1.call-done), kind=kLoop, calls=%fused_computation.2 | loop fusion | flops 6291456 | bytes 8388608 | tf_op jit(solution)/shard_map/convert_element_type | solution.py:59
  (3 shorter events, 0.0 us)
Async XLA Ops:
  7.2 41.9 %copy-start = (bf16[256,4096]{1,0:T(8,128)(2,1)S(1)}, bf16[256,4096]{1,0:T(8,128)(2,1)}, u32[]{:S(2)}) copy-start(bf16[256,4096]{1,0:T(8,128)(2,1)} %param.2) | copy-start | bytes 6291460
  7.2 37.1 %all-gather.10.cloned.1.call-start = ((), (), s32[]{:S(2)}) async-start(), calls=%async_computation.8 | async-start | bytes 1310720 | tf_op jit(solution)/shard_map/all_gather | solution.py:28
  9.1 83.8 %all-reduce.3.cloned.1.call-start = ((), (), s32[]{:S(2)}) async-start(), calls=%async_computation.3 | async-start | bytes 262144 | tf_op jit(solution)/shard_map/psum | solution.py:30
  49.1 70.6 %reduce-scatter.3.cloned.1.call-start = ((), (), s32[]{:S(2)}) async-start(), calls=%async_computation.2 | async-start | bytes 327680 | tf_op jit(solution)/shard_map/reduce_scatter | solution.py:36
  53.3 190.3 %all-gather.6.cloned.1.call-start = ((), (), s32[]{:S(2)}) async-start(), calls=%async_computation.4 | async-start | bytes 8519680 | tf_op jit(solution)/shard_map/all_gather | solution.py:31
  92.9 191.8 %all-gather.8.cloned.1.call-start = ((), (), s32[]{:S(2)}) async-start(), calls=%async_computation.5 | async-start | bytes 1310720 | tf_op jit(solution)/shard_map/all_gather | solution.py:45
  260.2 89.9 %reduce-scatter.5.cloned.1.call-start = ((), (), s32[]{:S(2)}) async-start(), calls=%async_computation.6 | async-start | bytes 2228224 | tf_op jit(solution)/shard_map/reduce_scatter | solution.py:51
  288.3 208.0 %all-reduce.5.cloned.1.call-start = ((), (), s32[]{:S(2)}) async-start(), calls=%async_computation.7 | async-start | bytes 8388608 | tf_op jit(solution)/shard_map/psum | solution.py:58
  350.1 2.7 copy-start.1
Sparse Core Ops, SparseCore 0:
  10.4 33.8 all-gather.9
  49.2 43.6 all-reduce.2
  96.2 23.4 reduce-scatter.2
  121.4 122.2 all-gather.5
  260.3 24.3 all-gather.7
  288.5 61.6 reduce-scatter.4
  356.4 139.8 all-reduce.4

commit v2 on v1

v2 whole, which is shorter than its diff:
```python
import functools
import math

import jax
import jax.numpy as jnp
from jax import lax
from jax.experimental import pallas as pl
from jax.experimental.pallas import tpu as pltpu
from jax.sharding import PartitionSpec as P

D = 16384
BF16 = jnp.bfloat16
F32 = jnp.float32
MESH = pl.DeviceIdType.MESH
ROWS = 256
WIDTH = 4096
BLOCK = 512
H = 256
SCALE = math.sqrt(D) / 4096


def dot(a, b, ca, cb):
    return lax.dot_general(a, b, (((ca,), (cb,)), ((), ())), preferred_element_type=F32)


def at(start, size):
    return pl.ds(pl.multiple_of(start, size), size)


def kernel(
    tokens, basis, out, proj,
    tok, tok_other, w, wz, tpart, trecv, tall, upart, urecv, u, q, gpart, grecv, gfull,
    ahalf, afull, az, s1, p2, xa, xb, xc, e2, zb,
    ssem, lsem, r_tok, r_w, r_t, r_ta, r_u, r_us, r_ux, r_uc, r_q, r_qc, r_g, r_ga,
    r_az, r_xa, r_xb, r_xc, r_zb, r_o1x, r_o1z, r_o2z, r_o2x, r_oc,
):
    s = lax.axis_index("section")
    d = lax.axis_index("dp")
    f = lax.axis_index("feat")
    x, z, c = d // 4, (d // 2) % 2, d % 2
    xz = d // 2
    zo, co = 1 - z, 1 - c

    def dev(s=s, x=x, z=z, c=c, f=f):
        return (s, x * 4 + z * 2 + c, f)

    pending = []

    def when(cond, do):
        if cond is None:
            do()
        else:
            pl.when(cond)(do)

    def send(src, dst, target, sem, cond=None):
        copy = pltpu.make_async_remote_copy(
            src_ref=src, dst_ref=dst, send_sem=ssem.at[len(pending)], recv_sem=sem,
            device_id=target, device_id_type=MESH,
        )
        when(cond, copy.start)
        pending.append((copy, cond))

    def arrived(dst, sem, cond=None):
        when(cond, pltpu.make_async_copy(dst, dst, sem).wait)

    feats = at((2 * c + z) * 1024, 1024)
    load_tok = pltpu.make_async_copy(tokens, tok, lsem.at[0])
    load_w = pltpu.make_async_copy(basis, w, lsem.at[1])
    load_z = pltpu.make_async_copy(basis.at[at(x * 128, 128), feats], wz.at[at(s * 128, 128)], lsem.at[2])
    load_tok.start()
    load_w.start()
    load_z.start()

    group = f * 4 + z * 2 + c
    sections = [dev(s=(s + k) % 4) for k in range(1, 4)]
    sixteen = []
    for k in range(1, 16):
        g = (group + k) % 16
        sixteen.append((g, dev(f=g // 4, z=(g // 2) % 2, c=g % 2)))
    planes = []
    for k in range(1, 8):
        p = (xz // 2 + k // 2) % 4 * 2 + (z + k) % 2
        planes.append((p, dev(x=p // 2, z=p % 2)))
    barrier = pltpu.get_barrier_semaphore()
    friends = sections + [t for _, t in sixteen] + [t for k, (_, t) in enumerate(planes, 1) if k // 2 > 0]
    for target in friends:
        pl.semaphore_signal(barrier, inc=1, device_id=target, device_id_type=MESH)
    for j in range(3):
        def clear(j=j):
            upart[j] = jnp.zeros((128, 512), BF16)
        pl.when(j >= s)(clear)
    for j in range(1, 4):
        def clear(j=j):
            wz[j * 128:(j + 1) * 128] = jnp.zeros((128, 1024), BF16)
        pl.when(j > s)(clear)
    pl.semaphore_wait(barrier, len(friends))

    for k in (3, 2, 1):
        send(basis.at[at(x * 128, 128), feats], wz.at[at(s * 128, 128)], dev(s=(s + k) % 4), r_w.at[s], s + k < 4)
    load_tok.wait()
    send(tok.at[:, at(co * 2048, 2048)], tok_other, dev(c=co), r_tok)
    load_w.wait()

    def score(t, carry):
        cols = at(t * 128, 128)
        tpart[:, cols] = dot(tok[...], w[cols, :], 1, 1).astype(BF16)
        return carry
    lax.fori_loop(0, 4, score, 0)
    for k in range(1, 4):
        g = (f + k) % 4
        send(tpart.at[:, at(g * 128, 128)], trecv.at[f], dev(f=g), r_t.at[f])
    total = tpart[:, at(f * 128, 128)].astype(F32)
    for k in range(1, 4):
        g = (f + k) % 4
        arrived(trecv.at[g], r_t.at[g])
        total = total + trecv[g].astype(F32)
    tall[s] = total.astype(BF16)
    for k in (3, 2, 1):
        send(tall.at[s], tall.at[s], dev(s=(s + k) % 4), r_ta.at[s], s + k < 4)

    load_z.wait()
    for j in range(3):
        def cross(j=j):
            arrived(wz.at[pl.ds(j * 128, 128)], r_w.at[j])
            upart[j] = dot(wz[j * 128:(j + 1) * 128], w[:, feats], 1, 1).astype(BF16)
        pl.when(j < s)(cross)
    some = s > 0
    for g, target in sixteen:
        send(upart.at[:, at(g % 4 * 32, 32), at(g // 4 * 128, 128)], urecv.at[group], target, r_u.at[group], some)

    def step(b):
        def do():
            arrived(tall.at[b], r_ta.at[b], b < s)
            y = tall[b].astype(F32)
            for j in range(b):
                y = y - dot(q[c, j], u[b * (b - 1) // 2 + j].reshape(BLOCK, 128), 1, 0)
            q[c, b, :, at(f * 128, 128)] = y.astype(BF16)
        need = b <= s
        pl.when(need)(do)
        for k in range(1, 4):
            mine = q.at[c, b, :, at(f * 128, 128)]
            send(mine, mine, dev(f=(f + k) % 4), r_q.at[b * 4 + f], need)
        for k in range(1, 4):
            g = (f + k) % 4
            arrived(q.at[c, b, :, at(g * 128, 128)], r_q.at[b * 4 + g], need)
        send(q.at[c, b], q.at[c, b], dev(c=co), r_qc.at[b], need)

    step(0)

    def reduce_cross():
        total = upart[:, at(group % 4 * 32, 32), at(f * 128, 128)].astype(F32)
        for g, _ in sixteen:
            arrived(urecv.at[g], r_u.at[g])
            total = total + urecv[g].astype(F32)
        total = total.astype(BF16)
        for b in range(1, 4):
            def put(b=b):
                for j in range(b):
                    u[b * (b - 1) // 2 + j, xz, c] = total[j]
            pl.when(s == b)(put)
    pl.when(some)(reduce_cross)
    one, two, three = u.at[pl.ds(0, 1), xz, c], u.at[pl.ds(1, 2), xz, c], u.at[pl.ds(0, 6), xz, c]
    send(one, one, dev(s=3), r_us.at[0], s == 1)
    send(one, one, dev(s=2), r_us.at[0], s == 1)
    send(two, two, dev(s=3), r_us.at[1], s == 2)
    arrived(one, r_us.at[0], s >= 2)
    arrived(two, r_us.at[1], s == 3)
    for b in range(1, 4):
        n = b * (b + 1) // 2
        for p, target in planes:
            mine = u.at[pl.ds(0, n), xz, c]
            send(mine, mine, target, r_ux.at[xz], s == b)
        for p, _ in planes:
            arrived(u.at[pl.ds(0, n), p, c], r_ux.at[p], s == b)
        both = u.at[pl.ds(0, n), :, c]
        send(both, both, dev(c=co), r_uc, s == b)
        arrived(u.at[pl.ds(0, n), :, co], r_uc, s == b)

    for b in range(1, 4):
        step(b)
    for b in range(4):
        arrived(q.at[co, b], r_qc.at[b], b <= s)
    proj[...] = q[c, s].astype(F32)

    for j in range(4):
        def gram(j=j):
            cols = at(f * 128, 128)
            g = dot(q[0, j], q[0, s, :, cols], 0, 0) + dot(q[1, j], q[1, s, :, cols], 0, 0)
            gpart[j] = g.astype(BF16).reshape(8, 2, 32, 128)
        pl.when(j <= s)(gram)

        def none(j=j):
            gpart[j] = jnp.zeros((8, 2, 32, 128), BF16)
        pl.when(j > s)(none)
    for p, target in planes:
        send(gpart.at[:, p, c], grecv.at[xz], target, r_g.at[xz])

    arrived(tok_other, r_tok)
    turned = [q[k, s].T for k in range(2)]
    mine_q = jnp.where(c == 0, turned[0], turned[1])
    other_q = jnp.where(c == 0, turned[1], turned[0])

    def hebb(t, half):
        here = dot(mine_q, tok[:, at(c * 2048 + half * 1024 + t * 256, 256)], 1, 0)
        there = dot(other_q, tok_other[:, at(half * 1024 + t * 256, 256)], 1, 0)
        return here + there

    def first(t, carry):
        ahalf[:, at(t * 256, 256)] = hebb(t, zo).astype(BF16)
        return carry
    lax.fori_loop(0, 4, first, 0)
    send(ahalf.at[pl.ds(0, H)], az, dev(z=zo), r_az)
    for k in range(1, 4):
        g = (x + k) % 4
        send(ahalf.at[pl.ds(H, BLOCK - H), at(g * 256, 256)], xb.at[x], dev(x=g), r_xb.at[x])

    def second(t, carry):
        afull[:, at(t * 256, 256)] = hebb(t, z)
        return carry
    lax.fori_loop(0, 4, second, 0)

    total = gpart[:, xz, c].astype(F32)
    for p, _ in planes:
        arrived(grecv.at[p], r_g.at[p])
        total = total + grecv[p].astype(F32)
    shape = (4, 32, 128)
    block = lax.broadcasted_iota(jnp.int32, shape, 0)
    col = d * 32 + lax.broadcasted_iota(jnp.int32, shape, 1)
    row = f * 128 + lax.broadcasted_iota(jnp.int32, shape, 2)
    keep = (block < s) | ((block == s) & (col <= row))
    gfull[:, at(group % 4 * 32, 32), at(f * 128, 128)] = jnp.where(keep, total, 0.0).astype(BF16)
    mine = gfull.at[:, at(group % 4 * 32, 32), at(f * 128, 128)]
    for g, target in sixteen:
        send(mine, mine, target, r_ga.at[group])
    for g, _ in sixteen:
        arrived(gfull.at[:, at(g % 4 * 32, 32), at(g // 4 * 128, 128)], r_ga.at[g])
    lower = gfull[...].reshape(512, BLOCK).T

    def damp(t, carry):
        cols = at(t * 256, 256)
        afull[:, cols] = afull[:, cols] - dot(lower, wz[:, cols], 1, 0)
        return carry
    lax.fori_loop(0, 4, damp, 0)

    mycols = at(x * 256, 256)
    p2[...] = afull[H:].astype(BF16)
    for k in range(1, 4):
        g = (x + k) % 4
        send(p2.at[:, at(g * 256, 256)], xc.at[x], dev(x=g), r_xc.at[x])
    arrived(az, r_az)
    afull[:H] = afull[:H] + az[...].astype(F32)
    s1[...] = afull[:H].astype(BF16)
    for k in range(1, 4):
        g = (x + k) % 4
        send(s1.at[:, at(g * 256, 256)], xa.at[x], dev(x=g), r_xa.at[x])
    total = ahalf[H:, mycols].astype(F32)
    for k in range(1, 4):
        g = (x + k) % 4
        arrived(xb.at[g], r_xb.at[g])
        total = total + xb[g].astype(F32)
    e2[...] = total.astype(BF16)
    send(e2, zb, dev(z=zo), r_zb)
    total = afull[H:, mycols]
    for k in range(1, 4):
        g = (x + k) % 4
        arrived(xc.at[g], r_xc.at[g])
        total = total + xc[g].astype(F32)
    arrived(zb, r_zb)
    total = total + zb[...].astype(F32)

    def cols_of(x, z, n=256):
        return at(c * 2048 + z * 1024 + x * 256, n)

    top, low = pl.ds(0, H), pl.ds(H, BLOCK - H)
    out[H:, cols_of(x, z)] = (total * SCALE).astype(BF16)
    mine = out.at[low, cols_of(x, z)]
    send(mine, mine, dev(z=zo), r_o2z)
    for k in range(1, 4):
        send(mine, mine, dev(x=(x + k) % 4), r_o2x.at[x])
    total = afull[:H, mycols]
    for k in range(1, 4):
        g = (x + k) % 4
        arrived(xa.at[g], r_xa.at[g])
        total = total + xa[g].astype(F32)
    out[:H, cols_of(x, z)] = (total * SCALE).astype(BF16)
    mine = out.at[top, cols_of(x, z)]
    for k in range(1, 4):
        send(mine, mine, dev(x=(x + k) % 4), r_o1x.at[x])
    other = out.at[low, cols_of(x, zo)]
    arrived(other, r_o2z)
    for k in range(1, 4):
        send(other, other, dev(x=(x + k) % 4), r_o2x.at[4 + x])
    for k in range(1, 4):
        g = (x + k) % 4
        arrived(out.at[top, cols_of(g, z)], r_o1x.at[g])
    mine = out.at[top, at(c * 2048 + z * 1024, 1024)]
    send(mine, mine, dev(z=zo), r_o1z)
    send(mine, mine, dev(c=co), r_oc.at[0])
    for k in range(1, 4):
        g = (x + k) % 4
        arrived(out.at[low, cols_of(g, z)], r_o2x.at[g])
    mine = out.at[low, at(c * 2048 + z * 1024, 1024)]
    send(mine, mine, dev(c=co), r_oc.at[1])
    for k in range(1, 4):
        g = (x + k) % 4
        arrived(out.at[low, cols_of(g, zo)], r_o2x.at[4 + g])
    mine = out.at[low, at(c * 2048 + zo * 1024, 1024)]
    send(mine, mine, dev(c=co), r_oc.at[2])
    mine = out.at[top, at(c * 2048 + zo * 1024, 1024)]
    arrived(mine, r_o1z)
    send(mine, mine, dev(c=co), r_oc.at[3])
    arrived(out.at[top, at(co * 2048 + z * 1024, 1024)], r_oc.at[0])
    arrived(out.at[low, at(co * 2048 + z * 1024, 1024)], r_oc.at[1])
    arrived(out.at[low, at(co * 2048 + zo * 1024, 1024)], r_oc.at[2])
    arrived(out.at[top, at(co * 2048 + zo * 1024, 1024)], r_oc.at[3])
    for copy, cond in pending:
        when(cond, copy.wait_send)


def shards(tokens, basis):
    dma = pltpu.SemaphoreType.DMA
    vm = pltpu.VMEM
    out, proj = pl.pallas_call(
        kernel,
        out_shape=(
            jax.ShapeDtypeStruct((BLOCK, WIDTH), BF16),
            jax.ShapeDtypeStruct((ROWS, BLOCK), F32),
        ),
        in_specs=[pl.BlockSpec(memory_space=pl.ANY)] * 2,
        out_specs=(pl.BlockSpec(memory_space=pltpu.VMEM), pl.BlockSpec(memory_space=pltpu.VMEM)),
        scratch_shapes=[
            vm((ROWS, WIDTH), BF16),
            vm((ROWS, 2048), BF16),
            vm((BLOCK, WIDTH), BF16),
            vm((512, 1024), BF16),
            vm((ROWS, BLOCK), BF16),
            vm((4, ROWS, 128), BF16),
            vm((4, ROWS, 128), BF16),
            vm((3, 128, 512), BF16),
            vm((16, 3, 32, 128), BF16),
            vm((6, 8, 2, 32, 128), BF16),
            vm((2, 4, ROWS, BLOCK), BF16),
            vm((4, 8, 2, 32, 128), BF16),
            vm((8, 4, 32, 128), BF16),
            vm((4, 128, 512), BF16),
            vm((BLOCK, 1024), BF16),
            vm((BLOCK, 1024), F32),
            vm((H, 1024), BF16),
            vm((H, 1024), BF16),
            vm((BLOCK - H, 1024), BF16),
            vm((4, H, 256), BF16),
            vm((4, BLOCK - H, 256), BF16),
            vm((4, BLOCK - H, 256), BF16),
            vm((BLOCK - H, 256), BF16),
            vm((BLOCK - H, 256), BF16),
            dma((160,)),
            dma((3,)),
            dma,
            dma((4,)),
            dma((4,)),
            dma((4,)),
            dma((16,)),
            dma((2,)),
            dma((8,)),
            dma,
            dma((16,)),
            dma((4,)),
            dma((8,)),
            dma((16,)),
            dma,
            dma((4,)),
            dma((4,)),
            dma((4,)),
            dma,
            dma((4,)),
            dma,
            dma,
            dma((8,)),
            dma((4,)),
        ],
        compiler_params=pltpu.CompilerParams(
            collective_id=0, has_side_effects=True, vmem_limit_bytes=56 << 20
        ),
        name="sanger",
    )(tokens, basis)
    return out, proj


def solution(mesh):
    in_specs = (P("dp", "feat"), P("section", "feat"))
    out_specs = (P("section", "feat"), P("dp", "section"))
    return jax.shard_map(shards, mesh=mesh, in_specs=in_specs, out_specs=out_specs, check_vma=False)
```

time: 517 us -> 146 us (0.28); the launches traced: 508 us -> 146 us
  waiting for transfers between devices: 439 us -> 0 us
  Pallas kernels: 0 us -> 140 us
  matrix products: 24.5 us -> 0 us
  between operations: 14.2 us -> 0.65 us
  blocking collectives: 11.6 us -> 0 us
  other arithmetic: 6.85 us -> 0 us
  local copies, waits for them, and re-layouts: 11.7 us -> 5.55 us
    psum x2 -> x0, waiting for transfers between devices: 179 us -> none  [the longest x1 139 us: shards(): total = lax.psum(part.astype(BF16), 'dp')]
    all_gather x3 -> x0, waiting for transfers between devices: 172 us -> none  [the longest x1 112 us: shards(): cross = lax.all_gather(cross, ('section', 'dp'))]
    pallas_call x0 -> x1, Pallas kernels: none -> 140 us  [shards(): pl.pallas_call(kernel, out_shape=(jax.ShapeDtypeStruct((BLOCK, WIDTH), BF...]
    reduce_scatter x2 -> x0, waiting for transfers between devices: 88.4 us -> none  [the longest x1 61.7 us: shards(): gram = lax.psum_scatter(gram, 'dp', scatter_dimension=0, tiled=True)[0]]
    dot_general x11 -> x0, matrix products: 24.5 us -> none  [the longest x10 22.5 us: dot(): lax.dot_general(a, b, (((ca,), (cb,)), ((), ())), preferred_element_type=...]
    all_gather x1 -> x0, blocking collectives: 11.6 us -> none  [shards(): scores = lax.all_gather(scores, 'section')]
    transpose x1 -> x0, local copies, waits for them, and re-layouts: 8.28 us -> none  [shards(): cross = cross.transpose(0, 2, 1, 3, 4).reshape(n_sec, n_sec, block, block)]
    convert_element_type x2 -> x0, other arithmetic: 6.09 us -> none  [the longest x1 5.23 us: shards(): basis_step = (total.astype(F32) * scaling).astype(BF16)]
  transfers between devices with their start and end apart: 7 -> 0, of which waited for: 7 -> 0; matrix products, arithmetic and copies ran while one was open for 1% -> 0% of each run, Pallas kernels for 0% -> 0%
where the time goes in v2:
time: 146 us
  Pallas kernels  140 us (96%)
  local copies, waits for them, and re-layouts  5.55 us (4%)
    pallas_call x1, Pallas kernels, shards(): pl.pallas_call(kernel, out_shape=(jax.ShapeDtypeStruct((BLOCK, WIDTH), BF...  140 us
    unnamed x4, local copies, waits for them, and re-layouts  5.55 us

profile of v2, /device:TPU:225, one launch (start us, length us, event | category | flops | bytes accessed | tf_op | source)
XLA Modules:
  0.0 146.1 jit_solution(11947649644718315036)
XLA Ops:
  0.6 139.9 %sanger.1 = (bf16[512,4096]{1,0:T(8,128)(2,1)}, f32[256,512]{1,0:T(8,128)}) custom-call(bf16[256,4096]{1,0:T(8,128)(2,1)} %tokens.1, bf16[512,4096]{1,0:T(8,128)(2,1)} %basis.1), custom_call_target="tpu_custom_call" | custom-call | tf_op jit(solution)/shard_map/sanger/pallas_call | solution.py:323
  140.5 0.0 copy-start
  140.5 4.8 %copy.6 = bf16[512,4096]{1,0:T(8,128)(2,1)} copy(bf16[512,4096]{1,0:T(8,128)(2,1)} %get-tuple-element.4) | data formatting | bytes 8388608
  145.3 0.0 copy-done
  145.3 0.8 copy.7
Async XLA Ops:
  140.5 4.8 %copy-start = (f32[256,512]{1,0:T(8,128)S(1)}, f32[256,512]{1,0:T(8,128)}, u32[]{:S(2)}) copy-start(f32[256,512]{1,0:T(8,128)} %get-tuple-element.5) | copy-start | bytes 1572868

commit v3 on v2

--- a/solution.py
+++ b/solution.py
@@ -15,7 +15,8 @@
 ROWS = 256
 WIDTH = 4096
 BLOCK = 512
-H = 256
+H = 128
+TOP = 224
 SCALE = math.sqrt(D) / 4096
 
 
@@ -32,7 +33,7 @@
     tok, tok_other, w, wz, tpart, trecv, tall, upart, urecv, u, q, gpart, grecv, gfull,
     ahalf, afull, az, s1, p2, xa, xb, xc, e2, zb,
     ssem, lsem, r_tok, r_w, r_t, r_ta, r_u, r_us, r_ux, r_uc, r_q, r_qc, r_g, r_ga,
-    r_az, r_xa, r_xb, r_xc, r_zb, r_o1x, r_o1z, r_o2z, r_o2x, r_oc,
+    r_az, r_xa, r_xb, r_xc, r_zb, r_ox, r_oz, r_oc, r_w0,
 ):
     s = lax.axis_index("section")
     d = lax.axis_index("dp")
@@ -95,8 +96,11 @@
         pl.when(j > s)(clear)
     pl.semaphore_wait(barrier, len(friends))
 
-    for k in (3, 2, 1):
-        send(basis.at[at(x * 128, 128), feats], wz.at[at(s * 128, 128)], dev(s=(s + k) % 4), r_w.at[s], s + k < 4)
+    for n in range(4):
+        for b in (3, 1):
+            send(basis.at[at(x * 128 + n * 32, 32), feats], wz.at[pl.ds(n * 32, 32)], dev(s=b), r_w0.at[n], s == 0)
+    for k in (2, 1):
+        send(basis.at[at(x * 128, 128), feats], wz.at[at(s * 128, 128)], dev(s=(s + k) % 4), r_w.at[s], (s > 0) & (s + k < 4))
     load_tok.wait()
     send(tok.at[:, at(co * 2048, 2048)], tok_other, dev(c=co), r_tok)
     load_w.wait()
@@ -115,37 +119,51 @@
         arrived(trecv.at[g], r_t.at[g])
         total = total + trecv[g].astype(F32)
     tall[s] = total.astype(BF16)
-    for k in (3, 2, 1):
-        send(tall.at[s], tall.at[s], dev(s=(s + k) % 4), r_ta.at[s], s + k < 4)
 
     load_z.wait()
+    for n in range(4):
+        part = wz.at[pl.ds(n * 32, 32)]
+        arrived(part, r_w0.at[n], s > 0)
+        send(part, part, dev(s=2), r_w0.at[n], s == 3)
     for j in range(3):
         def cross(j=j):
-            arrived(wz.at[pl.ds(j * 128, 128)], r_w.at[j])
+            if j > 0:
+                arrived(wz.at[pl.ds(j * 128, 128)], r_w.at[j])
             upart[j] = dot(wz[j * 128:(j + 1) * 128], w[:, feats], 1, 1).astype(BF16)
         pl.when(j < s)(cross)
     some = s > 0
     for g, target in sixteen:
         send(upart.at[:, at(g % 4 * 32, 32), at(g // 4 * 128, 128)], urecv.at[group], target, r_u.at[group], some)
 
-    def step(b):
+    for k in (3, 2, 1):
+        send(tall.at[s], tall.at[s], dev(s=(s + k) % 4), r_ta.at[s], s + k < 4)
+
+    def step(b, h):
+        rows = pl.ds(h * 128, 128)
+        need = b <= s
+
         def do():
-            arrived(tall.at[b], r_ta.at[b], b < s)
-            y = tall[b].astype(F32)
+            if h == 0:
+                arrived(tall.at[b], r_ta.at[b], b < s)
+            y = tall[b, rows].astype(F32)
             for j in range(b):
-                y = y - dot(q[c, j], u[b * (b - 1) // 2 + j].reshape(BLOCK, 128), 1, 0)
-            q[c, b, :, at(f * 128, 128)] = y.astype(BF16)
+                y = y - dot(q[c, j, rows], u[b * (b - 1) // 2 + j].reshape(BLOCK, 128), 1, 0)
+            q[c, b, rows, at(f * 128, 128)] = y.astype(BF16)
+        pl.when(need)(do)
+        mine = q.at[c, b, rows, at(f * 128, 128)]
+        for k in range(1, 4):
+            send(mine, mine, dev(f=(f + k) % 4), r_q.at[(b * 2 + h) * 4 + f], need)
+
+    def complete(b, h):
+        rows = pl.ds(h * 128, 128)
         need = b <= s
-        pl.when(need)(do)
-        for k in range(1, 4):
-            mine = q.at[c, b, :, at(f * 128, 128)]
-            send(mine, mine, dev(f=(f + k) % 4), r_q.at[b * 4 + f], need)
         for k in range(1, 4):
             g = (f + k) % 4
-            arrived(q.at[c, b, :, at(g * 128, 128)], r_q.at[b * 4 + g], need)
-        send(q.at[c, b], q.at[c, b], dev(c=co), r_qc.at[b], need)
-
-    step(0)
+            arrived(q.at[c, b, rows, at(g * 128, 128)], r_q.at[(b * 2 + h) * 4 + g], need)
+        send(q.at[c, b, rows], q.at[c, b, rows], dev(c=co), r_qc.at[b * 2 + h], need)
+
+    step(0, 0)
+    step(0, 1)
 
     def reduce_cross():
         total = upart[:, at(group % 4 * 32, 32), at(f * 128, 128)].astype(F32)
@@ -176,10 +194,14 @@
         send(both, both, dev(c=co), r_uc, s == b)
         arrived(u.at[pl.ds(0, n), :, co], r_uc, s == b)
 
-    for b in range(1, 4):
-        step(b)
+    for b in range(1, 5):
+        for h in range(2):
+            complete(b - 1, h)
+            if b < 4:
+                step(b, h)
     for b in range(4):
-        arrived(q.at[co, b], r_qc.at[b], b <= s)
+        for h in range(2):
+            arrived(q.at[co, b, pl.ds(h * 128, 128)], r_qc.at[b * 2 + h], b <= s)
     proj[...] = q[c, s].astype(F32)
 
     for j in range(4):
@@ -271,48 +293,81 @@
     def cols_of(x, z, n=256):
         return at(c * 2048 + z * 1024 + x * 256, n)
 
-    top, low = pl.ds(0, H), pl.ds(H, BLOCK - H)
     out[H:, cols_of(x, z)] = (total * SCALE).astype(BF16)
-    mine = out.at[low, cols_of(x, z)]
-    send(mine, mine, dev(z=zo), r_o2z)
-    for k in range(1, 4):
-        send(mine, mine, dev(x=(x + k) % 4), r_o2x.at[x])
     total = afull[:H, mycols]
     for k in range(1, 4):
         g = (x + k) % 4
         arrived(xa.at[g], r_xa.at[g])
         total = total + xa[g].astype(F32)
     out[:H, cols_of(x, z)] = (total * SCALE).astype(BF16)
-    mine = out.at[top, cols_of(x, z)]
-    for k in range(1, 4):
-        send(mine, mine, dev(x=(x + k) % 4), r_o1x.at[x])
-    other = out.at[low, cols_of(x, zo)]
-    arrived(other, r_o2z)
-    for k in range(1, 4):
-        send(other, other, dev(x=(x + k) % 4), r_o2x.at[4 + x])
-    for k in range(1, 4):
-        g = (x + k) % 4
-        arrived(out.at[top, cols_of(g, z)], r_o1x.at[g])
-    mine = out.at[top, at(c * 2048 + z * 1024, 1024)]
-    send(mine, mine, dev(z=zo), r_o1z)
-    send(mine, mine, dev(c=co), r_oc.at[0])
-    for k in range(1, 4):
-        g = (x + k) % 4
-        arrived(out.at[low, cols_of(g, z)], r_o2x.at[g])
-    mine = out.at[low, at(c * 2048 + z * 1024, 1024)]
-    send(mine, mine, dev(c=co), r_oc.at[1])
-    for k in range(1, 4):
-        g = (x + k) % 4
-        arrived(out.at[low, cols_of(g, zo)], r_o2x.at[4 + g])
-    mine = out.at[low, at(c * 2048 + zo * 1024, 1024)]
-    send(mine, mine, dev(c=co), r_oc.at[2])
-    mine = out.at[top, at(c * 2048 + zo * 1024, 1024)]
-    arrived(mine, r_o1z)
-    send(mine, mine, dev(c=co), r_oc.at[3])
-    arrived(out.at[top, at(co * 2048 + z * 1024, 1024)], r_oc.at[0])
-    arrived(out.at[low, at(co * 2048 + z * 1024, 1024)], r_oc.at[1])
-    arrived(out.at[low, at(co * 2048 + zo * 1024, 1024)], r_oc.at[2])
-    arrived(out.at[top, at(co * 2048 + zo * 1024, 1024)], r_oc.at[3])
+
+    right, left, far = (x + 1) % 4, (x + 3) % 4, (x + 2) % 4
+    top, low = (0, TOP), (TOP, BLOCK - TOP)
+    kinds = ((top, z), (low, z), (low, zo))
+    cores = []
+
+    def piece(rows, gx, gz, half=None, gc=c):
+        start, size = rows
+        if half is not None:
+            start, size = start + half * (size // 2), size // 2
+        return out.at[pl.ds(start, size), at(gc * 2048 + gz * 1024 + gx * 256, 256)]
+
+    def to_core(rows, gx, gz, half=None):
+        ref = piece(rows, gx, gz, half)
+        send(ref, ref, dev(c=co), r_oc.at[len(cores)])
+        cores.append((rows, gx, gz, half))
+
+    def round_x(i):
+        ref = piece(kinds[i][0], x, kinds[i][1])
+        send(ref, ref, dev(x=right), r_ox.at[i * 4])
+        send(ref, ref, dev(x=left), r_ox.at[i * 4 + 1])
+
+    def pass_on(i):
+        rows, gz = kinds[i]
+        for g, half, to, n in ((left, 0, right, 0), (right, 1, left, 1)):
+            arrived(piece(rows, g, gz), r_ox.at[i * 4 + n])
+            ref = piece(rows, g, gz, half)
+            send(ref, ref, dev(x=to), r_ox.at[i * 4 + 2 + n])
+            if i == 0:
+                over_z(g)
+            to_core(rows, g, gz)
+
+    def last(i):
+        rows, gz = kinds[i]
+        for half in range(2):
+            arrived(piece(rows, far, gz, half), r_ox.at[i * 4 + 2 + half])
+            if i == 0:
+                over_z(far, half)
+            to_core(rows, far, gz, half)
+
+    overs = []
+
+    def over_z(g, half=None):
+        ref = piece(top, g, z, half)
+        send(ref, ref, dev(z=zo), r_oz.at[len(overs)])
+        overs.append((g, half))
+
+    mine = piece(low, x, z)
+    send(mine, mine, dev(z=zo), r_oz.at[5])
+    round_x(1)
+    round_x(0)
+    over_z(x)
+    to_core(low, x, z)
+    to_core(top, x, z)
+    arrived(piece(low, x, zo), r_oz.at[5])
+    round_x(2)
+    to_core(low, x, zo)
+    pass_on(0)
+    pass_on(1)
+    pass_on(2)
+    last(0)
+    last(1)
+    last(2)
+    for n, (g, half) in enumerate(overs):
+        arrived(piece(top, g, zo, half), r_oz.at[n])
+        to_core(top, g, zo, half)
+    for n, (rows, gx, gz, half) in enumerate(cores):
+        arrived(piece(rows, gx, gz, half, co), r_oc.at[n])
     for copy, cond in pending:
         when(cond, copy.wait_send)
 
@@ -323,8 +378,8 @@
     out, proj = pl.pallas_call(
         kernel,
         out_shape=(
-            jax.ShapeDtypeStruct((BLOCK, WIDTH), BF16),
-            jax.ShapeDtypeStruct((ROWS, BLOCK), F32),
+            pltpu.VMEM((BLOCK, WIDTH), BF16),
+            pltpu.VMEM((ROWS, BLOCK), F32),
         ),
         in_specs=[pl.BlockSpec(memory_space=pl.ANY)] * 2,
         out_specs=(pl.BlockSpec(memory_space=pltpu.VMEM), pl.BlockSpec(memory_space=pltpu.VMEM)),
@@ -353,7 +408,7 @@
             vm((4, BLOCK - H, 256), BF16),
             vm((BLOCK - H, 256), BF16),
             vm((BLOCK - H, 256), BF16),
-            dma((160,)),
+            dma((220,)),
             dma((3,)),
             dma,
             dma((4,)),
@@ -363,8 +418,8 @@
             dma((2,)),
             dma((8,)),
             dma,
-            dma((16,)),
-            dma((4,)),
+            dma((32,)),
+            dma((8,)),
             dma((8,)),
             dma((16,)),
             dma,
@@ -372,10 +427,9 @@
             dma((4,)),
             dma((4,)),
             dma,
-            dma((4,)),
-            dma,
-            dma,
-            dma((8,)),
+            dma((12,)),
+            dma((6,)),
+            dma((24,)),
             dma((4,)),
         ],
         compiler_params=pltpu.CompilerParams(

time: 146 us -> 125 us (0.86)
  Pallas kernels: 140 us -> 122 us
  local copies, waits for them, and re-layouts: 5.55 us -> 2.81 us
    pallas_call x1, Pallas kernels: 140 us -> 122 us  [shards(): pl.pallas_call(kernel, out_shape=(pltpu.VMEM((BLOCK, WIDTH), BF16), pltpu...]
    unnamed x4 -> x2, local copies, waits for them, and re-layouts: 5.55 us -> 2.81 us
where the time goes in v3:
time: 125 us
  Pallas kernels  122 us (98%)
  local copies, waits for them, and re-layouts  2.81 us (2%)
    pallas_call x1, Pallas kernels, shards(): pl.pallas_call(kernel, out_shape=(pltpu.VMEM((BLOCK, WIDTH), BF16), pltpu...  122 us
    unnamed x2, local copies, waits for them, and re-layouts  2.81 us

profile of v3, /device:TPU:225, one launch (start us, length us, event | category | flops | bytes accessed | tf_op | source)
XLA Modules:
  0.0 125.2 jit_solution(15051256352114499583)
XLA Ops:
  0.6 121.7 %sanger.1 = (bf16[512,4096]{1,0:T(8,128)(2,1)S(1)}, f32[256,512]{1,0:T(8,128)S(1)}) custom-call(bf16[256,4096]{1,0:T(8,128)(2,1)} %tokens.1, bf16[512,4096]{1,0:T(8,128)(2,1)} %basis.1), custom_call_target="tpu_custom_call" | custom-call | tf_op jit(solution)/shard_map/sanger/pallas_call | solution.py:378
  122.4 2.0 %copy.6 = bf16[512,4096]{1,0:T(8,128)(2,1)} copy(bf16[512,4096]{1,0:T(8,128)(2,1)S(1)} %get-tuple-element.2) | data formatting | bytes 8388608
  124.4 0.8 copy.7

commit v4 on v3

v4 whole, which is shorter than its diff:
```python
import functools
import math

import jax
import jax.numpy as jnp
from jax import lax
from jax.experimental import pallas as pl
from jax.experimental.pallas import tpu as pltpu
from jax.sharding import PartitionSpec as P

D = 16384
BF16 = jnp.bfloat16
F32 = jnp.float32
MESH = pl.DeviceIdType.MESH
ROWS = 256
WIDTH = 4096
BLOCK = 512
PARTS = 2
PART = ROWS // PARTS
H = 64
TOP = 256
SCALE = math.sqrt(D) / 4096


def dot(a, b, ca, cb):
    return lax.dot_general(a, b, (((ca,), (cb,)), ((), ())), preferred_element_type=F32)


def at(start, size):
    return pl.ds(pl.multiple_of(start, size), size)


def kernel(
    tokens, basis, out, proj,
    tok, tok_other, w, wz, tpart, trecv, tall, upart, ucore, usum, urecv, u, q, gpart, grecv, gfull, turned,
    ahalf, afull, az, s1, p2, xa, oa, sa, xb, ob, sb, xc, oc, sc, e2, zb,
    ssem, lsem, r_tok, r_w, r_t, r_ta, r_u, r_us, r_ux, r_uc, r_q, r_qc, r_g, r_ga,
    r_az, r_xa, r_xb, r_xc, r_zb, r_ox, r_oz, r_oc, r_w0, r_uh, r_gc,
):
    s = lax.axis_index("section")
    d = lax.axis_index("dp")
    f = lax.axis_index("feat")
    x, z, c = d // 4, (d // 2) % 2, d % 2
    xz = d // 2
    zo, co = 1 - z, 1 - c

    def dev(s=s, x=x, z=z, c=c, f=f):
        return (s, x * 4 + z * 2 + c, f)

    pending = []
    bufs_a, bufs_b, bufs_c = (xa, oa, sa), (xb, ob, sb), (xc, oc, sc)

    def when(cond, do):
        if cond is None:
            do()
        else:
            pl.when(cond)(do)

    def send(src, dst, target, sem, cond=None):
        copy = pltpu.make_async_remote_copy(
            src_ref=src, dst_ref=dst, send_sem=ssem.at[len(pending)], recv_sem=sem,
            device_id=target, device_id_type=MESH,
        )
        when(cond, copy.start)
        pending.append((copy, cond))

    def arrived(dst, sem, cond=None):
        when(cond, pltpu.make_async_copy(dst, dst, sem).wait)

    feats = at((2 * c + z) * 1024, 1024)
    load_tok = pltpu.make_async_copy(tokens, tok, lsem.at[0])
    load_w = pltpu.make_async_copy(basis, w, lsem.at[1])
    load_z = pltpu.make_async_copy(basis.at[at(x * 128, 128), feats], wz.at[at(s * 128, 128)], lsem.at[2])
    load_tok.start()
    load_w.start()
    load_z.start()

    group = f * 4 + z * 2 + c
    sections = [dev(s=(s + k) % 4) for k in range(1, 4)]
    eight = []
    for k in range(1, 8):
        g = (f + k // 2) % 4 * 2 + (z + k) % 2
        eight.append((g, dev(f=g // 2, z=g % 2)))
    planes = []
    for k in range(1, 8):
        p = (xz // 2 + k // 2) % 4 * 2 + (z + k) % 2
        planes.append((p, dev(x=p // 2, z=p % 2)))
    barrier = pltpu.get_barrier_semaphore()
    friends = sections + [dev(c=co)] + [t for _, t in eight] + [t for k, (_, t) in enumerate(planes, 1) if k // 2 > 0]
    for target in friends:
        pl.semaphore_signal(barrier, inc=1, device_id=target, device_id_type=MESH)
    for j in range(3):
        def clear(j=j):
            upart[j] = jnp.zeros((2, 2, 32, 512), BF16)
        pl.when(j >= s)(clear)
    for j in range(1, 4):
        def clear(j=j):
            wz[j * 128:(j + 1) * 128] = jnp.zeros((128, 1024), BF16)
        pl.when(j > s)(clear)
    pl.semaphore_wait(barrier, len(friends))

    def slice_zero(n):
        for b in (3, 1):
            send(basis.at[at(x * 128 + n * 32, 32), feats], wz.at[pl.ds(n * 32, 32)], dev(s=b), r_w0.at[n], s == 0)

    def relay(n, cond):
        part = wz.at[pl.ds(n * 32, 32)]
        arrived(part, r_w0.at[n], cond)
        send(part, part, dev(s=2), r_w0.at[n], s == 3)

    slice_zero(0)
    def slice_on(k, cond):
        send(basis.at[at(x * 128, 128), feats], wz.at[at(s * 128, 128)], dev(s=(s + k) % 4), r_w.at[s], cond)

    slice_on(1, (s == 1) | (s == 2))
    load_tok.wait()
    send(tok.at[:, at(co * 2048, 2048)], tok_other, dev(c=co), r_tok)
    load_w.wait()

    def score(t, carry):
        cols = at(t * 128, 128)
        tpart[:, cols] = dot(tok[...], w[cols, :], 1, 1).astype(BF16)
        return carry
    lax.fori_loop(0, 4, score, 0)
    slice_zero(1)
    for k in range(1, 4):
        g = (f + k) % 4
        send(tpart.at[:, at(g * 128, 128)], trecv.at[f], dev(f=g), r_t.at[f])
    slice_zero(2)
    for n in range(2):
        relay(n, s == 3)
    total = tpart[:, at(f * 128, 128)].astype(F32)
    for k in range(1, 4):
        g = (f + k) % 4
        arrived(trecv.at[g], r_t.at[g])
        total = total + trecv[g].astype(F32)
    slice_zero(3)
    slice_on(2, s == 1)
    tall[s] = total.astype(BF16)

    load_z.wait()
    for n in range(2):
        arrived(wz.at[pl.ds(n * 32, 32)], r_w0.at[n], (s > 0) & (s < 3))
    for n in range(2, 4):
        relay(n, s > 0)
    for j in range(3):
        def cross(j=j):
            if j > 0:
                arrived(wz.at[pl.ds(j * 128, 128)], r_w.at[j])
            upart[j] = dot(wz[j * 128:(j + 1) * 128], w[:, feats], 1, 1).astype(BF16).reshape(2, 2, 32, 512)
        pl.when(j < s)(cross)
    some = s > 0
    send(upart.at[:, :, co], ucore, dev(c=co), r_uh, some)

    def add_core():
        arrived(ucore, r_uh)
        usum[...] = (upart[:, :, c].astype(F32) + ucore[...].astype(F32)).astype(BF16)
    pl.when(some)(add_core)
    for g, target in eight:
        send(usum.at[:, g % 2, :, at(g // 2 * 128, 128)], urecv.at[f * 2 + z], target, r_u.at[f * 2 + z], some)

    for k in (3, 2, 1):
        send(tall.at[s], tall.at[s], dev(s=(s + k) % 4), r_ta.at[s], s + k < 4)

    def step(b, h):
        rows = pl.ds(h * PART, PART)
        need = b <= s

        def do():
            if h == 0:
                arrived(tall.at[b], r_ta.at[b], b < s)
            y = tall[b, rows].astype(F32)
            for j in range(b):
                y = y - dot(q[c, j, rows], u[b * (b - 1) // 2 + j].reshape(BLOCK, 128), 1, 0)
            q[c, b, rows, at(f * 128, 128)] = y.astype(BF16)
        pl.when(need)(do)
        mine = q.at[c, b, rows, at(f * 128, 128)]
        for k in range(1, 4):
            send(mine, mine, dev(f=(f + k) % 4), r_q.at[(b * PARTS + h) * 4 + f], need)

    def complete(b, h):
        rows = pl.ds(h * PART, PART)
        need = b <= s
        for k in range(1, 4):
            g = (f + k) % 4
            arrived(q.at[c, b, rows, at(g * 128, 128)], r_q.at[(b * PARTS + h) * 4 + g], need)
        send(q.at[c, b, rows], q.at[c, b, rows], dev(c=co), r_qc.at[b * PARTS + h], need)

    def reduce_cross():
        total = usum[:, z, :, at(f * 128, 128)].astype(F32)
        for g, _ in eight:
            arrived(urecv.at[g], r_u.at[g])
            total = total + urecv[g].astype(F32)
        total = total.astype(BF16)
        for b in range(1, 4):
            def put(b=b):
                for j in range(b):
                    u[b * (b - 1) // 2 + j, xz, c] = total[j]
            pl.when(s == b)(put)
    pl.when(some)(reduce_cross)

    def column(k, of, gc=None):
        return u.at[pl.ds(k * (k - 1) // 2, k), of, c if gc is None else gc]

    def spread(k, cond):
        for _, target in planes:
            send(column(k, xz), column(k, xz), target, r_ux.at[k * 8 + xz], cond)

    def to_core(k, cond):
        for p, _ in planes:
            arrived(column(k, p), r_ux.at[k * 8 + p], cond)
        both = column(k, slice(None))
        send(both, both, dev(c=co), r_uc.at[k], cond)

    def ready(k):
        arrived(column(k, slice(None), co), r_uc.at[k], s >= k)

    send(column(1, xz), column(1, xz), dev(s=3), r_us.at[1], s == 1)
    send(column(2, xz), column(2, xz), dev(s=3), r_us.at[2], s == 2)
    send(column(1, xz), column(1, xz), dev(s=2), r_us.at[1], s == 1)
    for k in range(1, 4):
        spread(k, s == k)
    arrived(column(1, xz), r_us.at[1], s >= 2)
    spread(1, s >= 2)
    for h in range(PARTS):
        step(0, h)
    to_core(1, s >= 1)
    for k in range(2, 4):
        to_core(k, s == k)
    for b in range(1, 5):
        if b == 2:
            arrived(column(2, xz), r_us.at[2], s == 3)
            spread(2, s == 3)
            to_core(2, s == 3)
        if b < 4:
            ready(b)
        for h in range(PARTS):
            complete(b - 1, h)
            if b < 4:
                step(b, h)
    for b in range(4):
        for h in range(PARTS):
            arrived(q.at[co, b, pl.ds(h * PART, PART)], r_qc.at[b * PARTS + h], b <= s)
    proj[...] = q[c, s].astype(F32)

    for k in range(2):
        turned[k] = q[k, s].T
    for j in range(4):
        def gram(j=j):
            rows = at(f * 128, 128)
            g = dot(turned[0, rows], q[0, j], 1, 0) + dot(turned[1, rows], q[1, j], 1, 0)
            gpart[j] = g.astype(BF16)
        pl.when(j <= s)(gram)

        def none(j=j):
            gpart[j] = jnp.zeros((128, BLOCK), BF16)
        pl.when(j > s)(none)
    for p, target in planes:
        mine = gpart.at[:, at((p % 2 * 2 + c) * 32, 32), at(p // 2 * 128, 128)]
        send(mine, grecv.at[xz], target, r_g.at[xz])

    mycols = at(x * 256, 256)
    arrived(tok_other, r_tok)

    def hebb(t, half):
        here = dot(turned[c], tok[:, at(c * 2048 + half * 1024 + t * 256, 256)], 1, 0)
        there = dot(turned[co], tok_other[:, at(half * 1024 + t * 256, 256)], 1, 0)
        return here + there

    right, left, far = (x + 1) % 4, (x + 3) % 4, (x + 2) % 4

    def block_of(ref, start, size, g):
        return ref.at[pl.ds(start, size), at(g * 256, 256)]

    def sum_start(src, start, size, bufs, sems):
        half = size // 2
        passing, sides = bufs[0], bufs[2]
        for to, n in ((right, 0), (left, 1)):
            send(block_of(src, start + n * half, half, far), passing.at[n], dev(x=to), sems.at[n])
        for to, n in ((right, 0), (left, 1)):
            m = 1 - n
            send(block_of(src, start + m * half, half, to), sides.at[n, pl.ds(m * half, half)], dev(x=to), sems.at[2 + n])

    def sum_pass(src, start, size, bufs, sems):
        half = size // 2
        passing, onward, sides = bufs
        for to, n in ((right, 0), (left, 1)):
            arrived(passing.at[n], sems.at[n])
            more = block_of(src, start + n * half, half, to)[...].astype(F32) + passing[n].astype(F32)
            onward[n] = more.astype(BF16)
            send(onward.at[n], sides.at[n, pl.ds(n * half, half)], dev(x=to), sems.at[4 + n])

    def sum_end(size, bufs, sems):
        half = size // 2
        sides = bufs[2]
        for n in range(2):
            arrived(sides.at[n, pl.ds((1 - n) * half, half)], sems.at[2 + n])
            arrived(sides.at[n, pl.ds(n * half, half)], sems.at[4 + n])
        return sides[0].astype(F32) + sides[1].astype(F32)

    def first(t, carry):
        ahalf[:, at(t * 256, 256)] = hebb(t, zo).astype(BF16)
        return carry
    lax.fori_loop(0, 4, first, 0)
    send(ahalf.at[pl.ds(0, H)], az, dev(z=zo), r_az)
    sum_start(ahalf, H, BLOCK - H, bufs_b, r_xb)

    total = gpart[:, at(group % 4 * 32, 32), at(x * 128, 128)].astype(F32)
    for p, _ in planes:
        arrived(grecv.at[p], r_g.at[p])
        total = total + grecv[p].astype(F32)
    shape = (4, 32, 128)
    block = lax.broadcasted_iota(jnp.int32, shape, 0)
    row = group * 32 + lax.broadcasted_iota(jnp.int32, shape, 1)
    col = x * 128 + lax.broadcasted_iota(jnp.int32, shape, 2)
    keep = (block < s) | ((block == s) & (col <= row))
    mine = gfull.at[:, at(group * 32, 32)]
    mine[...] = jnp.where(keep, total, 0.0).astype(BF16)
    for _, target in eight:
        send(mine, mine, target, r_ga.at[f * 2 + z])
    send(mine, mine, dev(c=co), r_gc.at[f * 2 + z])

    def second(t, carry):
        afull[:, at(t * 256, 256)] = hebb(t, z)
        return carry
    lax.fori_loop(0, 4, second, 0)

    sum_pass(ahalf, H, BLOCK - H, bufs_b, r_xb)
    for g, _ in eight:
        mine = gfull.at[:, at((g * 2 + c) * 32, 32)]
        arrived(mine, r_ga.at[g])
        send(mine, mine, dev(c=co), r_gc.at[g])
    for g in range(8):
        arrived(gfull.at[:, at((g * 2 + co) * 32, 32)], r_gc.at[g])

    def damp(start, size):
        rows = pl.ds(start, size)

        def tile(t, carry):
            cols = at(t * 256, 256)
            sums = afull[rows, cols]
            for j in range(4):
                sums = sums - dot(gfull[j, rows], wz[j * 128:(j + 1) * 128, cols], 1, 0)
            afull[rows, cols] = sums
            return carry
        lax.fori_loop(0, 4, tile, 0)

    damp(0, H)
    arrived(az, r_az)
    afull[:H] = afull[:H] + az[...].astype(F32)
    s1[...] = afull[:H].astype(BF16)
    sum_start(s1, 0, H, bufs_a, r_xa)
    e2[...] = (ahalf[H:, mycols].astype(F32) + sum_end(BLOCK - H, bufs_b, r_xb)).astype(BF16)
    send(e2, zb, dev(z=zo), r_zb)
    damp(H, BLOCK - H)
    p2[...] = afull[H:].astype(BF16)
    sum_pass(afull, 0, H, bufs_a, r_xa)
    sum_start(p2, 0, BLOCK - H, bufs_c, r_xc)

    def cols_of(x, z, n=256):
        return at(c * 2048 + z * 1024 + x * 256, n)

    total = afull[:H, mycols] + sum_end(H, bufs_a, r_xa)
    out[:H, cols_of(x, z)] = (total * SCALE).astype(BF16)

    sum_pass(afull, H, BLOCK - H, bufs_c, r_xc)
    arrived(zb, r_zb)
    total = afull[H:, mycols] + zb[...].astype(F32) + sum_end(BLOCK - H, bufs_c, r_xc)
    out[H:, cols_of(x, z)] = (total * SCALE).astype(BF16)
    top, low = (0, TOP), (TOP, BLOCK - TOP)
    kinds = ((top, z), (low, z), (low, zo))
    cores = []

    def piece(rows, gx, gz, half=None, gc=c):
        start, size = rows
        if half is not None:
            start, size = start + half * (size // 2), size // 2
        return out.at[pl.ds(start, size), at(gc * 2048 + gz * 1024 + gx * 256, 256)]

    def across(rows, gx, gz, half=None):
        ref = piece(rows, gx, gz, half)
        send(ref, ref, dev(c=co), r_oc.at[len(cores)])
        cores.append((rows, gx, gz, half))

    def round_x(i):
        ref = piece(kinds[i][0], x, kinds[i][1])
        send(ref, ref, dev(x=right), r_ox.at[i * 4])
        send(ref, ref, dev(x=left), r_ox.at[i * 4 + 1])

    def pass_on(i):
        rows, gz = kinds[i]
        for g, half, to, n in ((left, 0, right, 0), (right, 1, left, 1)):
            arrived(piece(rows, g, gz), r_ox.at[i * 4 + n])
            ref = piece(rows, g, gz, half)
            send(ref, ref, dev(x=to), r_ox.at[i * 4 + 2 + n])
            if i == 0:
                over_z(g)
            across(rows, g, gz)

    def last(i):
        rows, gz = kinds[i]
        for half in range(2):
            arrived(piece(rows, far, gz, half), r_ox.at[i * 4 + 2 + half])
            if i == 0:
                over_z(far, half)
            across(rows, far, gz, half)

    overs = []

    def over_z(g, half=None):
        ref = piece(top, g, z, half)
        send(ref, ref, dev(z=zo), r_oz.at[len(overs)])
        overs.append((g, half))

    mine = piece(low, x, z)
    send(mine, mine, dev(z=zo), r_oz.at[5])
    round_x(0)
    over_z(x)
    round_x(1)
    across(top, x, z)
    across(low, x, z)
    pass_on(0)
    arrived(piece(low, x, zo), r_oz.at[5])
    round_x(2)
    across(low, x, zo)
    pass_on(1)
    pass_on(2)
    last(0)
    last(1)
    last(2)
    for n, (g, half) in enumerate(overs):
        arrived(piece(top, g, zo, half), r_oz.at[n])
        across(top, g, zo, half)
    for n, (rows, gx, gz, half) in enumerate(cores):
        arrived(piece(rows, gx, gz, half, co), r_oc.at[n])
    for sent in pending:
        if sent is not None:
            when(sent[1], sent[0].wait_send)


def shards(tokens, basis):
    dma = pltpu.SemaphoreType.DMA
    vm = pltpu.VMEM
    out, proj = pl.pallas_call(
        kernel,
        out_shape=(
            pltpu.VMEM((BLOCK, WIDTH), BF16),
            pltpu.VMEM((ROWS, BLOCK), F32),
        ),
        in_specs=[pl.BlockSpec(memory_space=pl.ANY)] * 2,
        out_specs=(pl.BlockSpec(memory_space=pltpu.VMEM), pl.BlockSpec(memory_space=pltpu.VMEM)),
        scratch_shapes=[
            vm((ROWS, WIDTH), BF16),
            vm((ROWS, 2048), BF16),
            vm((BLOCK, WIDTH), BF16),
            vm((512, 1024), BF16),
            vm((ROWS, BLOCK), BF16),
            vm((4, ROWS, 128), BF16),
            vm((4, ROWS, 128), BF16),
            vm((3, 2, 2, 32, 512), BF16),
            vm((3, 2, 32, 512), BF16),
            vm((3, 2, 32, 512), BF16),
            vm((8, 3, 32, 128), BF16),
            vm((6, 8, 2, 32, 128), BF16),
            vm((2, 4, ROWS, BLOCK), BF16),
            vm((4, 128, BLOCK), BF16),
            vm((8, 4, 32, 128), BF16),
            vm((4, BLOCK, 128), BF16),
            vm((2, BLOCK, ROWS), BF16),
            vm((BLOCK, 1024), BF16),
            vm((BLOCK, 1024), F32),
            vm((H, 1024), BF16),
            vm((H, 1024), BF16),
            vm((BLOCK - H, 1024), BF16),
            vm((2, H // 2, 256), BF16),
            vm((2, H // 2, 256), BF16),
            vm((2, H, 256), BF16),
            vm((2, (BLOCK - H) // 2, 256), BF16),
            vm((2, (BLOCK - H) // 2, 256), BF16),
            vm((2, BLOCK - H, 256), BF16),
            vm((2, (BLOCK - H) // 2, 256), BF16),
            vm((2, (BLOCK - H) // 2, 256), BF16),
            vm((2, BLOCK - H, 256), BF16),
            vm((BLOCK - H, 256), BF16),
            vm((BLOCK - H, 256), BF16),
            dma((300,)),
            dma((3,)),
            dma,
            dma((4,)),
            dma((4,)),
            dma((4,)),
            dma((16,)),
            dma((4,)),
            dma((32,)),
            dma((4,)),
            dma((16 * PARTS,)),
            dma((4 * PARTS,)),
            dma((8,)),
            dma((16,)),
            dma,
            dma((6,)),
            dma((6,)),
            dma((6,)),
            dma,
            dma((12,)),
            dma((6,)),
            dma((24,)),
            dma((4,)),
            dma,
            dma((8,)),
        ],
        compiler_params=pltpu.CompilerParams(
            collective_id=0, has_side_effects=True, vmem_limit_bytes=56 << 20
        ),
        name="sanger",
    )(tokens, basis)
    return out, proj


def solution(mesh):
    in_specs = (P("dp", "feat"), P("section", "feat"))
    out_specs = (P("section", "feat"), P("dp", "section"))
    return jax.shard_map(shards, mesh=mesh, in_specs=in_specs, out_specs=out_specs, check_vma=False)
```

time: 125 us -> 114 us (0.912)
  Pallas kernels: 122 us -> 111 us
    pallas_call x1, Pallas kernels: 122 us -> 111 us  [shards(): pl.pallas_call(kernel, out_shape=(pltpu.VMEM((BLOCK, WIDTH), BF16), pltpu...]
where the time goes in v4:
time: 114 us
  Pallas kernels  111 us (97%)
  local copies, waits for them, and re-layouts  2.81 us (2%)
    pallas_call x1, Pallas kernels, shards(): pl.pallas_call(kernel, out_shape=(pltpu.VMEM((BLOCK, WIDTH), BF16), pltpu...  111 us
    unnamed x2, local copies, waits for them, and re-layouts  2.81 us

profile of v4, /device:TPU:225, one launch (start us, length us, event | category | flops | bytes accessed | tf_op | source)
XLA Modules:
  0.0 114.0 jit_solution(5985935437931493457)
XLA Ops:
  0.6 110.5 %sanger.1 = (bf16[512,4096]{1,0:T(8,128)(2,1)S(1)}, f32[256,512]{1,0:T(8,128)S(1)}) custom-call(bf16[256,4096]{1,0:T(8,128)(2,1)} %tokens.1, bf16[512,4096]{1,0:T(8,128)(2,1)} %basis.1), custom_call_target="tpu_custom_call" | custom-call | tf_op jit(solution)/shard_map/sanger/pallas_call | solution.py:444
  111.2 2.0 %copy.6 = bf16[512,4096]{1,0:T(8,128)(2,1)} copy(bf16[512,4096]{1,0:T(8,128)(2,1)S(1)} %get-tuple-element.2) | data formatting | bytes 8388608
  113.2 0.8 copy.7

commit v5 on v4

--- a/solution.py
+++ b/solution.py
@@ -350,12 +350,13 @@
     afull[:H] = afull[:H] + az[...].astype(F32)
     s1[...] = afull[:H].astype(BF16)
     sum_start(s1, 0, H, bufs_a, r_xa)
+    damp(H, BLOCK - H)
+    p2[...] = afull[H:].astype(BF16)
+    sum_start(p2, 0, BLOCK - H, bufs_c, r_xc)
     e2[...] = (ahalf[H:, mycols].astype(F32) + sum_end(BLOCK - H, bufs_b, r_xb)).astype(BF16)
     send(e2, zb, dev(z=zo), r_zb)
-    damp(H, BLOCK - H)
-    p2[...] = afull[H:].astype(BF16)
     sum_pass(afull, 0, H, bufs_a, r_xa)
-    sum_start(p2, 0, BLOCK - H, bufs_c, r_xc)
+    sum_pass(afull, H, BLOCK - H, bufs_c, r_xc)
 
     def cols_of(x, z, n=256):
         return at(c * 2048 + z * 1024 + x * 256, n)
@@ -363,7 +364,6 @@
     total = afull[:H, mycols] + sum_end(H, bufs_a, r_xa)
     out[:H, cols_of(x, z)] = (total * SCALE).astype(BF16)
 
-    sum_pass(afull, H, BLOCK - H, bufs_c, r_xc)
     arrived(zb, r_zb)
     total = afull[H:, mycols] + zb[...].astype(F32) + sum_end(BLOCK - H, bufs_c, r_xc)
     out[H:, cols_of(x, z)] = (total * SCALE).astype(BF16)

time: 114 us -> 112 us (0.982)
  Pallas kernels: 111 us -> 109 us
    pallas_call x1, Pallas kernels: 111 us -> 109 us  [shards(): pl.pallas_call(kernel, out_shape=(pltpu.VMEM((BLOCK, WIDTH), BF16), pltpu...]
where the time goes in v5:
time: 112 us
  Pallas kernels  109 us (97%)
  local copies, waits for them, and re-layouts  2.81 us (3%)
    pallas_call x1, Pallas kernels, shards(): pl.pallas_call(kernel, out_shape=(pltpu.VMEM((BLOCK, WIDTH), BF16), pltpu...  109 us
    unnamed x2, local copies, waits for them, and re-layouts  2.81 us

profile of v5, /device:TPU:225, one launch (start us, length us, event | category | flops | bytes accessed | tf_op | source)
XLA Modules:
  0.0 112.1 jit_solution(442276778303512652)
XLA Ops:
  0.6 108.6 %sanger.1 = (bf16[512,4096]{1,0:T(8,128)(2,1)S(1)}, f32[256,512]{1,0:T(8,128)S(1)}) custom-call(bf16[256,4096]{1,0:T(8,128)(2,1)} %tokens.1, bf16[512,4096]{1,0:T(8,128)(2,1)} %basis.1), custom_call_target="tpu_custom_call" | custom-call | tf_op jit(solution)/shard_map/sanger/pallas_call | solution.py:444
  109.3 2.0 %copy.6 = bf16[512,4096]{1,0:T(8,128)(2,1)} copy(bf16[512,4096]{1,0:T(8,128)(2,1)S(1)} %get-tuple-element.2) | data formatting | bytes 8388608
  111.3 0.8 copy.7

commit v6 on v5

--- a/solution.py
+++ b/solution.py
@@ -218,19 +218,19 @@
     send(column(1, xz), column(1, xz), dev(s=3), r_us.at[1], s == 1)
     send(column(2, xz), column(2, xz), dev(s=3), r_us.at[2], s == 2)
     send(column(1, xz), column(1, xz), dev(s=2), r_us.at[1], s == 1)
+    arrived(column(1, xz), r_us.at[1], s >= 2)
+    spread(1, s >= 2)
     for k in range(1, 4):
         spread(k, s == k)
-    arrived(column(1, xz), r_us.at[1], s >= 2)
-    spread(1, s >= 2)
     for h in range(PARTS):
         step(0, h)
     to_core(1, s >= 1)
-    for k in range(2, 4):
-        to_core(k, s == k)
+    to_core(2, s == 2)
     for b in range(1, 5):
         if b == 2:
             arrived(column(2, xz), r_us.at[2], s == 3)
             spread(2, s == 3)
+            to_core(3, s == 3)
             to_core(2, s == 3)
         if b < 4:
             ready(b)

time: 112 us -> 111 us (level)
  Pallas kernels: 109 us -> 107 us
    pallas_call x1, Pallas kernels: 109 us -> 107 us  [shards(): pl.pallas_call(kernel, out_shape=(pltpu.VMEM((BLOCK, WIDTH), BF16), pltpu...]
where the time goes in v6:
time: 111 us
  Pallas kernels  107 us (96%)
  local copies, waits for them, and re-layouts  2.81 us (3%)
    pallas_call x1, Pallas kernels, shards(): pl.pallas_call(kernel, out_shape=(pltpu.VMEM((BLOCK, WIDTH), BF16), pltpu...  107 us
    unnamed x2, local copies, waits for them, and re-layouts  2.81 us

profile of v6, /device:TPU:225, one launch (start us, length us, event | category | flops | bytes accessed | tf_op | source)
XLA Modules:
  0.0 110.5 jit_solution(14613952930752607197)
XLA Ops:
  0.6 107.1 %sanger.1 = (bf16[512,4096]{1,0:T(8,128)(2,1)S(1)}, f32[256,512]{1,0:T(8,128)S(1)}) custom-call(bf16[256,4096]{1,0:T(8,128)(2,1)} %tokens.1, bf16[512,4096]{1,0:T(8,128)(2,1)} %basis.1), custom_call_target="tpu_custom_call" | custom-call | tf_op jit(solution)/shard_map/sanger/pallas_call | solution.py:444
  107.7 2.0 %copy.6 = bf16[512,4096]{1,0:T(8,128)(2,1)} copy(bf16[512,4096]{1,0:T(8,128)(2,1)S(1)} %get-tuple-element.2) | data formatting | bytes 8388608
  109.8 0.8 copy.7
